TPU v7x, 256 devices: a whole 4x4x8 slice. The times are simulated.
256 devices in a mesh: store: 32 (over y, z), tp: 8 (over x, core).
Axes of the slice: x: 4, y: 4, z: 8, core: 2. Of those that a mesh axis runs over, the one named last changes fastest.
Arguments:
- queries: bfloat16 [32768, 8192], P('store', 'tp')
- fresh_kv: bfloat16 [2, 32768, 1024], P(None, ('store', 'tp'))
- page_pool: bfloat16 [2048, 2, 128, 1024], P('store', None, None, 'tp')
- page_host: int32 [128, 8], P('store'), may hold values from 0 to 31, as said below
- page_slot: int32 [128, 8], P('store'), may hold values from 0 to 63, as said below
- prefix_len: int32 [128], P('store'), may hold values from 513 to 1024
- fresh_len: int32 [32, 4], P('store'), may hold values from 1 to 384, 1024 in all within a row
Outputs:
- attention: bfloat16 [32768, 8192], P('store', 'tp')
Inputs may be any that keep to these rules, and one draw needn't show every extreme that they name: `page_host`: page p of request r is read only if p < ceil(prefix_len[r] / 128). Among the pages read by the 4 requests of one host, at most 2 lie on any one host; in every draw some host holds exactly 2 of the pages read by each host. `page_slot`: several entries may name the same stored page. `fresh_len`: the requests of a host own consecutive rows of its block, in order.
All inputs are finite; a program needn't handle non-finite values.
Results may differ from a plain program's by a relative error of at most 0.0041.
Values may be sent and summed in bfloat16 or wider, within the bound.
A program may use at most 128 MiB of HBM per device.

v0:
```python
import math
import jax
import jax.numpy as jnp
from jax import lax
from jax.sharding import PartitionSpec as P

HD = 128
REQ_HOST = 4
PAGE = 128
PAGES_MAX = 8
MOST_NEW = 384


def plan_requests(owners, slot_ids, prefix, stores, capacity):
    entry_count = owners.shape[0] * owners.shape[1]
    page_count = (prefix + PAGE - 1) // PAGE
    in_use = (jnp.arange(owners.shape[1], dtype=jnp.int32)[None, :] < page_count[:, None]).reshape(
        entry_count
    )
    flat_owners = owners.reshape(entry_count)
    flat_slots = slot_ids.reshape(entry_count)
    entries = jnp.arange(entry_count, dtype=jnp.int32)
    same_owner = (
        (flat_owners[:, None] == flat_owners[None, :])
        & in_use[None, :]
        & (entries[None, :] < entries[:, None])
    )
    owner_rank = jnp.sum(same_owner.astype(jnp.int32), axis=1)
    position = jnp.where(in_use, flat_owners * capacity + owner_rank, 0)
    target = jnp.arange(stores * capacity, dtype=jnp.int32)
    matches = (position[:, None] == target[None, :]) & in_use[:, None]
    buffer = jnp.sum(jnp.where(matches, flat_slots[:, None], 0), axis=0)
    return (buffer.reshape(stores, capacity), position)


def attend(q_rows, key_rows, value_rows, key_valid):
    scores = jnp.einsum("mkgd,nkd->kgmn", q_rows, key_rows, preferred_element_type=jnp.float32) * (
        1.0 / math.sqrt(HD)
    )
    row_top = jnp.max(jnp.where(key_valid, scores, -1e30), axis=-1, keepdims=True)
    weights = jnp.where(key_valid, jnp.exp(scores - row_top), 0.0)
    row_total = jnp.sum(weights, axis=-1)
    rounded = weights.astype(jnp.bfloat16)
    mixed_rows = jnp.einsum(
        "kgmn,nkd->mkgd", rounded, value_rows, preferred_element_type=jnp.float32
    )
    return (mixed_rows / jnp.transpose(row_total, (2, 0, 1))[..., None]).astype(jnp.bfloat16)


def local(queries, fresh_kv, page_pool, page_host, page_slot, prefix_len, fresh_len):
    stores = lax.axis_size("store")
    block_rows = queries.shape[0]
    head_width = page_pool.shape[3]
    kv_local = head_width // HD
    group_size = queries.shape[1] // head_width
    capacity = max(2, (REQ_HOST * PAGES_MAX + stores - 1) // stores)
    gathered = lax.all_gather(fresh_kv, "tp", axis=1, tiled=True)
    new_kv = lax.dynamic_slice_in_dim(gathered, lax.axis_index("tp") * head_width, head_width, 2)
    buffer, position = plan_requests(page_host, page_slot, prefix_len, stores, capacity)
    arrived = lax.all_to_all(
        jnp.take(
            page_pool,
            lax.all_to_all(buffer, "store", split_axis=0, concat_axis=0, tiled=True),
            axis=0,
        ),
        "store",
        split_axis=0,
        concat_axis=0,
        tiled=True,
    )
    flat_pages = arrived.reshape(stores * capacity, 2, PAGE, head_width)
    fetched = jnp.take(flat_pages, position, axis=0).reshape(
        REQ_HOST, PAGES_MAX, 2, PAGE, head_width
    )
    lengths = fresh_len[0]
    offsets = jnp.cumsum(lengths) - lengths
    positions = jnp.arange(MOST_NEW, dtype=jnp.int32)
    cache_index = jnp.arange(PAGES_MAX * PAGE, dtype=jnp.int32)
    output = jnp.zeros_like(queries)
    for request in range(REQ_HOST):
        offset = offsets[request]
        length = lengths[request]
        window_start = jnp.minimum(offset, block_rows - MOST_NEW)
        q_rows = lax.dynamic_slice_in_dim(queries, window_start, MOST_NEW, 0).reshape(
            MOST_NEW, kv_local, group_size, HD
        )
        new_rows = lax.dynamic_slice_in_dim(new_kv, window_start, MOST_NEW, 1).reshape(
            2, MOST_NEW, kv_local, HD
        )
        cached_keys = fetched[request, :, 0].reshape(PAGES_MAX * PAGE, kv_local, HD)
        cached_values = fetched[request, :, 1].reshape(PAGES_MAX * PAGE, kv_local, HD)
        key_rows = jnp.concatenate([cached_keys, new_rows[0]], axis=0)
        value_rows = jnp.concatenate([cached_values, new_rows[1]], axis=0)
        query_pos = window_start + positions
        cache_ok = jnp.broadcast_to(
            cache_index[None, :] < prefix_len[request], (MOST_NEW, PAGES_MAX * PAGE)
        )
        fresh_ok = (query_pos[None, :] >= offset) & (query_pos[None, :] <= query_pos[:, None])
        key_valid = jnp.concatenate([cache_ok, fresh_ok], axis=1)
        mixed_rows = attend(q_rows, key_rows, value_rows, key_valid).reshape(
            MOST_NEW, queries.shape[1]
        )
        row_ok = (query_pos >= offset) & (query_pos < offset + length)
        old_rows = lax.dynamic_slice_in_dim(output, window_start, MOST_NEW, 0)
        output = lax.dynamic_update_slice_in_dim(
            output, jnp.where(row_ok[:, None], mixed_rows, old_rows), window_start, 0
        )
    return output


def solution(mesh):
    placed = (
        P("store", "tp"),
        P(None, ("store", "tp"), None),
        P("store", None, None, "tp"),
        P("store", None),
        P("store", None),
        P("store"),
        P("store", None),
    )
    return jax.shard_map(
        local, mesh=mesh, in_specs=placed, out_specs=P("store", "tp"), check_vma=False
    )
```

profile of v0, /device:TPU:2, one launch (start us, length us, event | category | flops | bytes accessed | tf_op | source)
XLA Modules:
  0.0 311.5 jit_solution(1080985737066531450)
XLA Ops:
  9.4 21.1 %all_to_all.20 = s32[32,1,2]{2,1,0:T(1,128)S(1)} all-to-all(s32[32,1,2]{2,1,0:T(1,128)S(1)} %bitcast.273), channel_id=1, replica_groups=mesh['store'=32,'tp'=8] {'store'}, dimensions={0} | all-to-all | bytes 512 | tf_op jit(solution)/shard_map/all_to_all | solution.py:63
  30.9 5.3 %gather_fusion = bf16[64,2,128,128]{3,2,1,0:T(8,128)(2,1)} fusion(bf16[64,2,128,128]{3,2,1,0:T(8,128)(2,1)} %param.9, s32[1024]{0:T(1024)S(1)} %pad_clamp_fusion.1), kind=kCustom, calls=%fused_computation | custom fusion | bytes 8388864 | tf_op jit(solution)/shard_map/jit(_take)/gather | solution.py:61
  36.2 4.5 %broadcast_select_fusion = bf16[32,2,2,128,128]{4,3,2,1,0:T(8,128)(2,1)} fusion(bf16[32,2,2,128,128]{4,3,2,1,0:T(8,128)(2,1)} %bitcast.255, pred[32,2]{1,0:T(8,128)(4,1)S(1)} %copy.87), kind=kLoop, calls=%fused_computation.42 | loop fusion | flops 2097152 | bytes 8388672 | tf_op jit(solution)/shard_map/jit(_take)/select_n | solution.py:61
  40.7 4.9 %all-to-all-start.1 = ((bf16[32,2,2,128,128]{4,3,2,1,0:T(8,128)(2,1)}), bf16[32,2,2,128,128]{4,3,2,1,0:T(8,128)(2,1)}, u32[]{:S(2)}, u32[]{:S(2)}) async-start(bf16[32,2,2,128,128]{4,3,2,1,0:T(8,128)(2,1)} %broadcast_select_fusion), calls=%async_computation.1 | async-start | bytes 8388608 | tf_op jit(solution)/shard_map/all_to_all | solution.py:60
  72.7 10.4 %all-gather.2.cloned.1.call-done = bf16[2,1024,1024]{2,1,0:T(8,128)(2,1)} async-done(((bf16[2,128,1024]{2,1,0:T(8,128)(2,1)}), bf16[2,1024,1024]{2,1,0:T(8,128)(2,1)}) %all-gather.2.cloned.1.call-update) | async-done | bytes 4194320 | tf_op jit(solution)/shard_map/all_gather | solution.py:57
  83.1 2.8 dynamic-slice_bitcast_fusion.1
  88.9 52.7 %all-to-all-done.1 = bf16[32,2,2,128,128]{4,3,2,1,0:T(8,128)(2,1)} async-done(((bf16[32,2,2,128,128]{4,3,2,1,0:T(8,128)(2,1)}), bf16[32,2,2,128,128]{4,3,2,1,0:T(8,128)(2,1)}, u32[]{:S(2)}, u32[]{:S(2)}) %all-to-all-start.1) | async-done | bytes 4194336 | tf_op jit(solution)/shard_map/all_to_all | solution.py:60
  141.6 4.3 %gather_fusion.1 = bf16[32,2,128,128]{3,2,1,0:T(8,128)(2,1)} fusion(bf16[64,2,128,128]{3,2,1,0:T(8,128)(2,1)} %bitcast.9, s32[1024]{0:T(1024)S(1)} %pad_clamp_fusion), kind=kCustom, calls=%fused_computation.1 | custom fusion | bytes 4194432 | tf_op jit(solution)/shard_map/jit(_take)/gather | solution.py:72
  150.7 9.9 %fusion = (f32[8,384]{1,0:T(8,128)S(1)}, f32[1408,384,8]{1,0,2:T(8,128)}) fusion(pred[384,1408]{0,1:T(8,128)(4,1)S(1)} %pad_add_fusion.3, bf16[384,8,128]{0,2,1:T(8,128)(2,1)} %bitcast.260, bf16[384,1,128]{2,0,1:T(8,128)(2,1)} %get-tuple-element.9, bf16[1024,1,128]{2,0,1:T(8,128)(2,1)} %bitcast.264), kind=kOutput, calls=%fused_computation.4 | convolution fusion | flops 1120990208 | bytes 19001344 | tf_op jit(solution)/shard_map/mkgd,nkd->kgmn/dot_general | solution.py:37
  160.6 9.8 %fusion.18 = f32[8,384]{1,0:T(8,128)S(1)} fusion(f32[1408,384,8]{1,0,2:T(8,128)} %get-tuple-element.44, f32[8,384]{1,0:T(8,128)S(1)} %get-tuple-element.43, pred[384,1408]{0,1:T(8,128)(4,1)S(1)} %pad_add_fusion.3), kind=kLoop, calls=%fused_computation.28 | loop fusion | flops 17298432 | bytes 17866752 | tf_op jit(solution)/shard_map/reduce_sum | solution.py:42
  170.5 10.7 %fusion.36 = bf16[384,1,8,128]{0,3,2,1:T(8,128)(2,1)} fusion(f32[1408,384,8]{1,0,2:T(8,128)} %get-tuple-element.44, f32[8,384]{1,0:T(8,128)S(1)} %get-tuple-element.43, pred[384,1408]{0,1:T(8,128)(4,1)S(1)} %pad_add_fusion.3, f32[384,8]{0,1:T(8,128)S(1)} %bitcast.274, bf16[384,1,128]{0,2,1:T(8,128)(2,1)} %copy.109, bf16[1024,1,128]{0,2,1:T(8,128)(2,1)} %copy.125), kind=kOutput, calls=%fused_computation.49 | convolution fusion | flops 1126105088 | bytes 19013632 | tf_op jit(solution)/shard_map/kgmn,nkd->mkgd/dot_general | solution.py:44
  185.2 9.9 %fusion.3 = (f32[8,384]{1,0:T(8,128)S(1)}, f32[1408,384,8]{1,0,2:T(8,128)}) fusion(pred[384,1408]{0,1:T(8,128)(4,1)S(1)} %pad_add_fusion.2, bf16[384,8,128]{0,2,1:T(8,128)(2,1)} %bitcast.259, bf16[384,1,128]{2,0,1:T(8,128)(2,1)} %get-tuple-element.10, bf16[1024,1,128]{2,0,1:T(8,128)(2,1)} %bitcast.263), kind=kOutput, calls=%fused_computation.9 | convolution fusion | flops 1120990208 | bytes 19001344 | tf_op jit(solution)/shard_map/mkgd,nkd->kgmn/dot_general | solution.py:37
  195.2 9.4 %fusion.16 = f32[8,384]{1,0:T(8,128)S(1)} fusion(f32[1408,384,8]{1,0,2:T(8,128)} %get-tuple-element.42, f32[8,384]{1,0:T(8,128)S(1)} %get-tuple-element.41, pred[384,1408]{0,1:T(8,128)(4,1)S(1)} %pad_add_fusion.2), kind=kLoop, calls=%fused_computation.26 | loop fusion | flops 17298432 | bytes 17866752 | tf_op jit(solution)/shard_map/reduce_sum | solution.py:42
  204.6 10.8 %fusion.37 = bf16[384,1,8,128]{0,3,2,1:T(8,128)(2,1)} fusion(f32[1408,384,8]{1,0,2:T(8,128)} %get-tuple-element.42, f32[8,384]{1,0:T(8,128)S(1)} %get-tuple-element.41, pred[384,1408]{0,1:T(8,128)(4,1)S(1)} %pad_add_fusion.2, f32[384,8]{0,1:T(8,128)S(1)} %bitcast.275, bf16[384,1,128]{0,2,1:T(8,128)(2,1)S(1)} %copy-done.9, bf16[1024,1,128]{0,2,1:T(8,128)(2,1)} %copy.124), kind=kOutput, calls=%fused_computation.51 | convolution fusion | flops 1126105088 | bytes 19013632 | tf_op jit(solution)/shard_map/kgmn,nkd->mkgd/dot_general | solution.py:44
  218.6 8.9 %fusion.6 = (f32[8,384]{1,0:T(8,128)S(1)}, f32[1408,384,8]{1,0,2:T(8,128)}) fusion(pred[384,1408]{0,1:T(8,128)(4,1)S(1)} %pad_add_fusion.1, bf16[384,8,128]{0,2,1:T(8,128)(2,1)} %bitcast.258, bf16[384,1,128]{2,0,1:T(8,128)(2,1)S(1)} %copy-done.6, bf16[1024,1,128]{2,0,1:T(8,128)(2,1)S(1)} %bitcast.262), kind=kOutput, calls=%fused_computation.14 | convolution fusion | flops 1120990208 | bytes 19001344 | tf_op jit(solution)/shard_map/mkgd,nkd->kgmn/dot_general | solution.py:37
  227.5 9.5 %fusion.14 = f32[8,384]{1,0:T(8,128)S(1)} fusion(f32[1408,384,8]{1,0,2:T(8,128)} %get-tuple-element.40, f32[8,384]{1,0:T(8,128)S(1)} %get-tuple-element.39, pred[384,1408]{0,1:T(8,128)(4,1)S(1)} %pad_add_fusion.1), kind=kLoop, calls=%fused_computation.24 | loop fusion | flops 17298432 | bytes 17866752 | tf_op jit(solution)/shard_map/reduce_sum | solution.py:42
  237.0 9.7 %fusion.38 = bf16[384,1,8,128]{0,3,2,1:T(8,128)(2,1)S(1)} fusion(f32[1408,384,8]{1,0,2:T(8,128)} %get-tuple-element.40, f32[8,384]{1,0:T(8,128)S(1)} %get-tuple-element.39, pred[384,1408]{0,1:T(8,128)(4,1)S(1)} %pad_add_fusion.1, f32[384,8]{0,1:T(8,128)S(1)} %bitcast.276, bf16[384,1,128]{0,2,1:T(8,128)(2,1)S(1)} %copy-done.8, bf16[1024,1,128]{0,2,1:T(8,128)(2,1)} %copy.123), kind=kOutput, calls=%fused_computation.53 | convolution fusion | flops 1126105088 | bytes 19013632 | tf_op jit(solution)/shard_map/kgmn,nkd->mkgd/dot_general | solution.py:44
  248.1 7.9 %fusion.9 = (f32[8,384]{1,0:T(8,128)S(1)}, f32[1408,384,8]{1,0,2:T(8,128)}) fusion(pred[384,1408]{0,1:T(8,128)(4,1)S(1)} %pad_add_fusion, bf16[384,8,128]{0,2,1:T(8,128)(2,1)S(1)} %bitcast.257, bf16[384,1,128]{2,0,1:T(8,128)(2,1)S(1)} %copy-done.5, bf16[1024,1,128]{2,0,1:T(8,128)(2,1)S(1)} %bitcast.261), kind=kOutput, calls=%fused_computation.19 | convolution fusion | flops 1120990208 | bytes 19001344 | tf_op jit(solution)/shard_map/mkgd,nkd->kgmn/dot_general | solution.py:37
  256.0 9.4 %fusion.12 = f32[8,384]{1,0:T(8,128)S(1)} fusion(f32[1408,384,8]{1,0,2:T(8,128)} %get-tuple-element.38, f32[8,384]{1,0:T(8,128)S(1)} %get-tuple-element.37, pred[384,1408]{0,1:T(8,128)(4,1)S(1)} %pad_add_fusion), kind=kLoop, calls=%fused_computation.22 | loop fusion | flops 17298432 | bytes 17866752 | tf_op jit(solution)/shard_map/reduce_sum | solution.py:42
  265.5 9.7 %fusion.39 = bf16[384,1,8,128]{0,3,2,1:T(8,128)(2,1)S(1)} fusion(f32[1408,384,8]{1,0,2:T(8,128)} %get-tuple-element.38, f32[8,384]{1,0:T(8,128)S(1)} %get-tuple-element.37, pred[384,1408]{0,1:T(8,128)(4,1)S(1)} %pad_add_fusion, f32[384,8]{0,1:T(8,128)S(1)} %bitcast.277, bf16[384,1,128]{0,2,1:T(8,128)(2,1)S(1)} %copy-done.7, bf16[1024,1,128]{0,2,1:T(8,128)(2,1)S(1)} %copy.122), kind=kOutput, calls=%fused_computation.55 | convolution fusion | flops 1126105088 | bytes 19013632 | tf_op jit(solution)/shard_map/kgmn,nkd->mkgd/dot_general | solution.py:44
  276.7 5.6 %dynamic_update_slice.12 = bf16[1024,1024]{1,0:T(8,128)(2,1)S(1)} dynamic-update-slice(bf16[1024,1024]{1,0:T(8,128)(2,1)S(1)} %broadcast_in_dim.152, bf16[384,1024]{1,0:T(8,128)(2,1)} %broadcast_select_fusion.2, s32[]{:T(128)S(6)} %select_n.157, s32[]{:T(128)} %constant.116.clone.1) | dynamic-update-slice | bytes 1572868 | tf_op jit(solution)/shard_map/dynamic_update_slice | solution.py:105
  284.7 5.5 %dynamic_update_slice.13 = bf16[1024,1024]{1,0:T(8,128)(2,1)S(1)} dynamic-update-slice(bf16[1024,1024]{1,0:T(8,128)(2,1)S(1)} %dynamic_update_slice.12, bf16[384,1024]{1,0:T(8,128)(2,1)} %dynamic-slice_select_fusion.2, s32[]{:T(128)S(6)} %select_n.164, s32[]{:T(128)} %constant.116.clone.1) | dynamic-update-slice | bytes 1572868 | tf_op jit(solution)/shard_map/dynamic_update_slice | solution.py:105
  292.6 5.5 %dynamic_update_slice.14 = bf16[1024,1024]{1,0:T(8,128)(2,1)S(1)} dynamic-update-slice(bf16[1024,1024]{1,0:T(8,128)(2,1)S(1)} %dynamic_update_slice.13, bf16[384,1024]{1,0:T(8,128)(2,1)} %dynamic-slice_select_fusion.1, s32[]{:T(128)S(6)} %select_n.169, s32[]{:T(128)} %constant.116.clone.1) | dynamic-update-slice | bytes 1572868 | tf_op jit(solution)/shard_map/dynamic_update_slice | solution.py:105
  299.7 4.7 %dynamic_update_slice.15 = bf16[1024,1024]{1,0:T(8,128)(2,1)} dynamic-update-slice(bf16[1024,1024]{1,0:T(8,128)(2,1)} %copy-done, bf16[384,1024]{1,0:T(8,128)(2,1)} %dynamic-slice_select_fusion, s32[]{:T(128)S(6)} %select_n.174, s32[]{:T(128)} %constant.116.clone.1) | dynamic-update-slice | bytes 1572868 | tf_op jit(solution)/shard_map/dynamic_update_slice | solution.py:105
  (104 shorter events, 47.0 us)
Async XLA Ops:
  6.5 47.7 %copy-start.10 = (s32[4,8]{1,0:T(4,128)S(1)}, s32[4,8]{1,0:T(4,128)}, u32[]{:S(2)}) copy-start(s32[4,8]{1,0:T(4,128)} %param.10) | copy-start | bytes 388
  6.5 39.8 %copy-start.11 = (s32[1,4]{1,0:T(1,128)S(1)}, s32[1,4]{1,0:T(1,128)}, u32[]{:S(2)}) copy-start(s32[1,4]{1,0:T(1,128)} %param.13) | copy-start | bytes 52
  6.5 43.3 %copy-start.1 = (bf16[1024,1024]{1,0:T(8,128)(2,1)S(1)}, bf16[1024,1024]{1,0:T(8,128)(2,1)}, u32[]{:S(2)}) copy-start(bf16[1024,1024]{1,0:T(8,128)(2,1)} %param.7) | copy-start | bytes 6291460
  30.9 28.9 %copy-start.12 = (s32[4]{0:T(128)S(1)}, s32[4]{0:T(128)}, u32[]{:S(2)}) copy-start(s32[4]{0:T(128)} %param.12) | copy-start | bytes 52
  40.7 100.9 %all-to-all-start.1 = ((bf16[32,2,2,128,128]{4,3,2,1,0:T(8,128)(2,1)}), bf16[32,2,2,128,128]{4,3,2,1,0:T(8,128)(2,1)}, u32[]{:S(2)}, u32[]{:S(2)}) async-start(bf16[32,2,2,128,128]{4,3,2,1,0:T(8,128)(2,1)} %broadcast_select_fusion), calls=%async_computation.1 | async-start | bytes 8388608 | tf_op jit(solution)/shard_map/all_to_all | solution.py:60
  45.6 37.5 %all-gather.2.cloned.1.call-start = ((), (), s32[]{:S(2)}) async-start(), calls=%async_computation.2 | async-start | bytes 4718592 | tf_op jit(solution)/shard_map/all_gather | solution.py:57
  185.2 19.4 %copy-start.9 = (bf16[384,1,128]{0,2,1:T(8,128)(2,1)S(1)}, bf16[384,1,128]{0,2,1:T(8,128)(2,1)}, u32[]{:S(2)}) copy-start(bf16[384,1,128]{0,2,1:T(8,128)(2,1)} %copy.103) | copy-start | bytes 294916
  204.6 13.2 %copy-start.4 = (bf16[1,8,1,128,128]{4,3,2,1,0:T(8,128)(2,1)S(1)}, bf16[1,8,1,128,128]{4,3,2,1,0:T(8,128)(2,1)}, u32[]{:S(2)}) copy-start(bf16[1,8,1,128,128]{4,3,2,1,0:T(8,128)(2,1)} %get-tuple-element.18) | copy-start | bytes 786436
  204.6 14.0 %copy-start.6 = (bf16[384,1,128]{2,0,1:T(8,128)(2,1)S(1)}, bf16[384,1,128]{2,0,1:T(8,128)(2,1)}, u32[]{:S(2)}) copy-start(bf16[384,1,128]{2,0,1:T(8,128)(2,1)} %get-tuple-element.11) | copy-start | bytes 294916
  227.5 9.5 %copy-start.8 = (bf16[384,1,128]{0,2,1:T(8,128)(2,1)S(1)}, bf16[384,1,128]{0,2,1:T(8,128)(2,1)}, u32[]{:S(2)}) copy-start(bf16[384,1,128]{0,2,1:T(8,128)(2,1)} %copy.97) | copy-start | bytes 294916
  237.0 11.0 %copy-start.3 = (bf16[1,8,1,128,128]{4,3,2,1,0:T(8,128)(2,1)S(1)}, bf16[1,8,1,128,128]{4,3,2,1,0:T(8,128)(2,1)}, u32[]{:S(2)}) copy-start(bf16[1,8,1,128,128]{4,3,2,1,0:T(8,128)(2,1)} %get-tuple-element.20) | copy-start | bytes 786436
  237.0 11.1 %copy-start.5 = (bf16[384,1,128]{2,0,1:T(8,128)(2,1)S(1)}, bf16[384,1,128]{2,0,1:T(8,128)(2,1)}, u32[]{:S(2)}) copy-start(bf16[384,1,128]{2,0,1:T(8,128)(2,1)} %get-tuple-element.12) | copy-start | bytes 294916
  248.1 17.4 %copy-start.7 = (bf16[384,1,128]{0,2,1:T(8,128)(2,1)S(1)}, bf16[384,1,128]{0,2,1:T(8,128)(2,1)}, u32[]{:S(2)}) copy-start(bf16[384,1,128]{0,2,1:T(8,128)(2,1)} %copy.91) | copy-start | bytes 294916
  265.5 32.7 %copy-start.2 = (bf16[384,1024]{1,0:T(8,128)(2,1)S(1)}, bf16[384,1024]{1,0:T(8,128)(2,1)}, u32[]{:S(2)}) copy-start(bf16[384,1024]{1,0:T(8,128)(2,1)} %copy.113) | copy-start | bytes 2359300
  298.1 1.6 copy-start
Sparse Core Ops, SparseCore 0:
  48.3 34.8 all-gather.1
where the time goes:
time: 315 us; the launch traced here: 311 us
  matrix products  77.5 us (25%)
  waiting for transfers between devices  63.6 us (20%)
  local copies, waits for them, and re-layouts  62.7 us (20%)
  other arithmetic  60 us (19%)
  between operations  21.5 us (7%)
  blocking collectives  21.1 us (7%)
  starting transfers between devices  5.07 us (2%)
    all_to_all x1, waiting for transfers between devices, local(): lax.all_to_all(jnp.take(page_pool, lax.all_to_all(buffer, 'store', split_...  52.7 us
    dot_general x4, matrix products, attend(): jnp.einsum('kgmn,nkd->mkgd', rounded, value_rows, preferred_element_type=...  40.9 us
    reduce_sum x4, other arithmetic, attend(): row_total = jnp.sum(weights, axis=-1)  38.1 us
    dot_general x4, matrix products, attend(): jnp.einsum('mkgd,nkd->kgmn', q_rows, key_rows, preferred_element_type=jnp...  36.7 us
    dynamic_update_slice x4, local copies, waits for them, and re-layouts, local(): lax.dynamic_update_slice_in_dim(output, jnp.where(row_ok[:, None], mixed_...  21.4 us
    all_to_all x1, blocking collectives, local(): lax.all_to_all(buffer, 'store', split_axis=0, concat_axis=0, tiled=True)  21.1 us
    all_gather x1, waiting for transfers between devices, local(): gathered = lax.all_gather(fresh_kv, 'tp', axis=1, tiled=True)  10.4 us
    unnamed x30, local copies, waits for them, and re-layouts  7.46 us
  transfers between devices with their start and end apart: 2, of which 2 were waited for; matrix products, arithmetic and copies ran while one was open for 8% of the time, Pallas kernels for 0%

commit v1 on v0

--- a/solution.py
+++ b/solution.py
@@ -54,7 +54,9 @@
     kv_local = head_width // HD
     group_size = queries.shape[1] // head_width
     capacity = max(2, (REQ_HOST * PAGES_MAX + stores - 1) // stores)
-    gathered = lax.all_gather(fresh_kv, "tp", axis=1, tiled=True)
+    gathered = jnp.concatenate(
+        lax.all_to_all(jnp.stack([fresh_kv] * lax.axis_size("tp")), "tp", 0, 0), axis=1
+    )
     new_kv = lax.dynamic_slice_in_dim(gathered, lax.axis_index("tp") * head_width, head_width, 2)
     buffer, position = plan_requests(page_host, page_slot, prefix_len, stores, capacity)
     arrived = lax.all_to_all(

time: 315 us -> 350 us (1.11)
  waiting for transfers between devices: 63.6 us -> 102 us
  between operations: 21.5 us -> 8.03 us
  starting transfers between devices: 5.07 us -> 10.2 us
  local copies, waits for them, and re-layouts: 62.7 us -> 67.6 us
    all_to_all x0 -> x1, waiting for transfers between devices: none -> 38.1 us  [local(): lax.all_to_all(jnp.stack([fresh_kv] * lax.axis_size('tp')), 'tp', 0, 0)]
    all_to_all x1, waiting for transfers between devices: 52.7 us -> 63.6 us  [local(): lax.all_to_all(jnp.take(page_pool, lax.all_to_all(buffer, 'store', split_...]
    all_gather x1 -> x0, waiting for transfers between devices: 10.4 us -> none  [local(): gathered = lax.all_gather(fresh_kv, 'tp', axis=1, tiled=True)]
    all_to_all x0 -> x1, starting transfers between devices: none -> 5.15 us  [local(): lax.all_to_all(jnp.stack([fresh_kv] * lax.axis_size('tp')), 'tp', 0, 0)]
    another operation x0 -> x1, local copies, waits for them, and re-layouts: none -> 3.55 us  [local(): jnp.stack([fresh_kv] * lax.axis_size('tp'))]
  transfers between devices with their start and end apart: 2 -> 2, of which waited for: 2 -> 2; matrix products, arithmetic and copies ran while one was open for 8% -> 10% of each run, Pallas kernels for 0% -> 0%
where the time goes in v1:
time: 350 us; the launch traced here: 346 us
  waiting for transfers between devices  102 us (29%)
  matrix products  77.7 us (22%)
  local copies, waits for them, and re-layouts  67.6 us (19%)
  other arithmetic  59.6 us (17%)
  blocking collectives  21.1 us (6%)
  starting transfers between devices  10.2 us (3%)
  between operations  8.03 us (2%)
    all_to_all x1, waiting for transfers between devices, local(): lax.all_to_all(jnp.take(page_pool, lax.all_to_all(buffer, 'store', split_...  63.6 us
    dot_general x4, matrix products, attend(): jnp.einsum('kgmn,nkd->mkgd', rounded, value_rows, preferred_element_type=...  41.1 us
    all_to_all x1, waiting for transfers between devices, local(): lax.all_to_all(jnp.stack([fresh_kv] * lax.axis_size('tp')), 'tp', 0, 0)  38.1 us
    reduce_sum x4, other arithmetic, attend(): row_total = jnp.sum(weights, axis=-1)  37.9 us
    dot_general x4, matrix products, attend(): jnp.einsum('mkgd,nkd->kgmn', q_rows, key_rows, preferred_element_type=jnp...  36.6 us
    dynamic_update_slice x4, local copies, waits for them, and re-layouts, local(): lax.dynamic_update_slice_in_dim(output, jnp.where(row_ok[:, None], mixed_...  21.4 us
    all_to_all x1, blocking collectives, local(): lax.all_to_all(buffer, 'store', split_axis=0, concat_axis=0, tiled=True)  21.1 us
    unnamed x30, local copies, waits for them, and re-layouts  7.46 us
  transfers between devices with their start and end apart: 2, of which 2 were waited for; matrix products, arithmetic and copies ran while one was open for 10% of the time, Pallas kernels for 0%

profile of v1, /device:TPU:2, one launch (start us, length us, event | category | flops | bytes accessed | tf_op | source)
XLA Modules:
  0.0 345.9 jit_solution(2673775640052587035)
XLA Ops:
  2.8 21.1 %all_to_all.25 = s32[32,1,2]{2,1,0:T(1,128)S(1)} all-to-all(s32[32,1,2]{2,1,0:T(1,128)S(1)} %bitcast.276), channel_id=1, replica_groups=mesh['store'=32,'tp'=8] {'store'}, dimensions={0} | all-to-all | bytes 512 | tf_op jit(solution)/shard_map/all_to_all | solution.py:65
  27.4 5.1 %all-to-all-start.2 = ((bf16[8,2,128,1024]{3,2,1,0:T(8,128)(2,1)}), bf16[8,2,128,1024]{3,2,1,0:T(8,128)(2,1)}, u32[]{:S(2)}, u32[]{:S(2)}) async-start(bf16[8,2,128,1024]{3,2,1,0:T(8,128)(2,1)} %stack.2), calls=%async_computation.2 | async-start | bytes 8388608 | tf_op jit(solution)/shard_map/all_to_all | solution.py:58
  33.0 5.2 %gather_fusion = bf16[64,2,128,128]{3,2,1,0:T(8,128)(2,1)} fusion(bf16[64,2,128,128]{3,2,1,0:T(8,128)(2,1)} %param.9, s32[1024]{0:T(1024)S(1)} %pad_clamp_fusion.1), kind=kCustom, calls=%fused_computation | custom fusion | bytes 8388864 | tf_op jit(solution)/shard_map/jit(_take)/gather | solution.py:63
  38.2 4.5 %broadcast_select_fusion = bf16[32,2,2,128,128]{4,3,2,1,0:T(8,128)(2,1)} fusion(bf16[32,2,2,128,128]{4,3,2,1,0:T(8,128)(2,1)} %bitcast.257, pred[32,2]{1,0:T(8,128)(4,1)S(1)} %copy.88), kind=kLoop, calls=%fused_computation.42 | loop fusion | flops 2097152 | bytes 8388672 | tf_op jit(solution)/shard_map/jit(_take)/select_n | solution.py:63
  42.7 38.1 %all-to-all-done.2 = bf16[8,2,128,1024]{3,2,1,0:T(8,128)(2,1)} async-done(((bf16[8,2,128,1024]{3,2,1,0:T(8,128)(2,1)}), bf16[8,2,128,1024]{3,2,1,0:T(8,128)(2,1)}, u32[]{:S(2)}, u32[]{:S(2)}) %all-to-all-start.2) | async-done | bytes 4194336 | tf_op jit(solution)/shard_map/all_to_all | solution.py:58
  80.9 5.0 %all-to-all-start.1 = ((bf16[32,2,2,128,128]{4,3,2,1,0:T(8,128)(2,1)}), bf16[32,2,2,128,128]{4,3,2,1,0:T(8,128)(2,1)}, u32[]{:S(2)}, u32[]{:S(2)}) async-start(bf16[32,2,2,128,128]{4,3,2,1,0:T(8,128)(2,1)} %broadcast_select_fusion), calls=%async_computation.1 | async-start | bytes 8388608 | tf_op jit(solution)/shard_map/all_to_all | solution.py:62
  119.3 63.6 %all-to-all-done.1 = bf16[32,2,2,128,128]{4,3,2,1,0:T(8,128)(2,1)} async-done(((bf16[32,2,2,128,128]{4,3,2,1,0:T(8,128)(2,1)}), bf16[32,2,2,128,128]{4,3,2,1,0:T(8,128)(2,1)}, u32[]{:S(2)}, u32[]{:S(2)}) %all-to-all-start.1) | async-done | bytes 4194336 | tf_op jit(solution)/shard_map/all_to_all | solution.py:62
  182.9 4.3 %gather_fusion.1 = bf16[32,2,128,128]{3,2,1,0:T(8,128)(2,1)} fusion(bf16[64,2,128,128]{3,2,1,0:T(8,128)(2,1)} %bitcast.9, s32[1024]{0:T(1024)S(1)} %pad_clamp_fusion), kind=kCustom, calls=%fused_computation.1 | custom fusion | bytes 4194432 | tf_op jit(solution)/shard_map/jit(_take)/gather | solution.py:74
  192.0 9.9 %fusion = (f32[8,384]{1,0:T(8,128)S(1)}, f32[1408,384,8]{1,0,2:T(8,128)}) fusion(pred[384,1408]{0,1:T(8,128)(4,1)S(1)} %pad_add_fusion.3, bf16[384,8,128]{0,2,1:T(8,128)(2,1)} %bitcast.263, bf16[384,1,128]{2,0,1:T(8,128)(2,1)} %get-tuple-element.9, bf16[1024,1,128]{2,0,1:T(8,128)(2,1)} %bitcast.267), kind=kOutput, calls=%fused_computation.4 | convolution fusion | flops 1120990208 | bytes 19001344 | tf_op jit(solution)/shard_map/mkgd,nkd->kgmn/dot_general | solution.py:37
  201.9 9.6 %fusion.18 = f32[8,384]{1,0:T(8,128)S(1)} fusion(f32[1408,384,8]{1,0,2:T(8,128)} %get-tuple-element.44, f32[8,384]{1,0:T(8,128)S(1)} %get-tuple-element.43, pred[384,1408]{0,1:T(8,128)(4,1)S(1)} %pad_add_fusion.3), kind=kLoop, calls=%fused_computation.28 | loop fusion | flops 17298432 | bytes 17866752 | tf_op jit(solution)/shard_map/reduce_sum | solution.py:42
  211.6 10.7 %fusion.36 = bf16[384,1,8,128]{0,3,2,1:T(8,128)(2,1)} fusion(f32[1408,384,8]{1,0,2:T(8,128)} %get-tuple-element.44, f32[8,384]{1,0:T(8,128)S(1)} %get-tuple-element.43, pred[384,1408]{0,1:T(8,128)(4,1)S(1)} %pad_add_fusion.3, f32[384,8]{0,1:T(8,128)S(1)} %bitcast.277, bf16[384,1,128]{0,2,1:T(8,128)(2,1)} %copy.111, bf16[1024,1,128]{0,2,1:T(8,128)(2,1)} %copy.127), kind=kOutput, calls=%fused_computation.49 | convolution fusion | flops 1126105088 | bytes 19013632 | tf_op jit(solution)/shard_map/kgmn,nkd->mkgd/dot_general | solution.py:44
  226.3 9.9 %fusion.3 = (f32[8,384]{1,0:T(8,128)S(1)}, f32[1408,384,8]{1,0,2:T(8,128)}) fusion(pred[384,1408]{0,1:T(8,128)(4,1)S(1)} %pad_add_fusion.2, bf16[384,8,128]{0,2,1:T(8,128)(2,1)} %bitcast.262, bf16[384,1,128]{2,0,1:T(8,128)(2,1)} %get-tuple-element.10, bf16[1024,1,128]{2,0,1:T(8,128)(2,1)} %bitcast.266), kind=kOutput, calls=%fused_computation.9 | convolution fusion | flops 1120990208 | bytes 19001344 | tf_op jit(solution)/shard_map/mkgd,nkd->kgmn/dot_general | solution.py:37
  236.3 9.4 %fusion.16 = f32[8,384]{1,0:T(8,128)S(1)} fusion(f32[1408,384,8]{1,0,2:T(8,128)} %get-tuple-element.42, f32[8,384]{1,0:T(8,128)S(1)} %get-tuple-element.41, pred[384,1408]{0,1:T(8,128)(4,1)S(1)} %pad_add_fusion.2), kind=kLoop, calls=%fused_computation.26 | loop fusion | flops 17298432 | bytes 17866752 | tf_op jit(solution)/shard_map/reduce_sum | solution.py:42
  245.7 11.0 %fusion.37 = bf16[384,1,8,128]{0,3,2,1:T(8,128)(2,1)} fusion(f32[1408,384,8]{1,0,2:T(8,128)} %get-tuple-element.42, f32[8,384]{1,0:T(8,128)S(1)} %get-tuple-element.41, pred[384,1408]{0,1:T(8,128)(4,1)S(1)} %pad_add_fusion.2, f32[384,8]{0,1:T(8,128)S(1)} %bitcast.278, bf16[384,1,128]{0,2,1:T(8,128)(2,1)S(1)} %copy-done.9, bf16[1024,1,128]{0,2,1:T(8,128)(2,1)} %copy.126), kind=kOutput, calls=%fused_computation.51 | convolution fusion | flops 1126105088 | bytes 19013632 | tf_op jit(solution)/shard_map/kgmn,nkd->mkgd/dot_general | solution.py:44
  260.0 8.9 %fusion.6 = (f32[8,384]{1,0:T(8,128)S(1)}, f32[1408,384,8]{1,0,2:T(8,128)}) fusion(pred[384,1408]{0,1:T(8,128)(4,1)S(1)} %pad_add_fusion.1, bf16[384,8,128]{0,2,1:T(8,128)(2,1)} %bitcast.261, bf16[384,1,128]{2,0,1:T(8,128)(2,1)S(1)} %copy-done.6, bf16[1024,1,128]{2,0,1:T(8,128)(2,1)S(1)} %bitcast.265), kind=kOutput, calls=%fused_computation.14 | convolution fusion | flops 1120990208 | bytes 19001344 | tf_op jit(solution)/shard_map/mkgd,nkd->kgmn/dot_general | solution.py:37
  268.8 9.5 %fusion.14 = f32[8,384]{1,0:T(8,128)S(1)} fusion(f32[1408,384,8]{1,0,2:T(8,128)} %get-tuple-element.40, f32[8,384]{1,0:T(8,128)S(1)} %get-tuple-element.39, pred[384,1408]{0,1:T(8,128)(4,1)S(1)} %pad_add_fusion.1), kind=kLoop, calls=%fused_computation.24 | loop fusion | flops 17298432 | bytes 17866752 | tf_op jit(solution)/shard_map/reduce_sum | solution.py:42
  278.3 9.7 %fusion.38 = bf16[384,1,8,128]{0,3,2,1:T(8,128)(2,1)S(1)} fusion(f32[1408,384,8]{1,0,2:T(8,128)} %get-tuple-element.40, f32[8,384]{1,0:T(8,128)S(1)} %get-tuple-element.39, pred[384,1408]{0,1:T(8,128)(4,1)S(1)} %pad_add_fusion.1, f32[384,8]{0,1:T(8,128)S(1)} %bitcast.279, bf16[384,1,128]{0,2,1:T(8,128)(2,1)S(1)} %copy-done.8, bf16[1024,1,128]{0,2,1:T(8,128)(2,1)} %copy.125), kind=kOutput, calls=%fused_computation.53 | convolution fusion | flops 1126105088 | bytes 19013632 | tf_op jit(solution)/shard_map/kgmn,nkd->mkgd/dot_general | solution.py:44
  289.4 7.9 %fusion.9 = (f32[8,384]{1,0:T(8,128)S(1)}, f32[1408,384,8]{1,0,2:T(8,128)}) fusion(pred[384,1408]{0,1:T(8,128)(4,1)S(1)} %pad_add_fusion, bf16[384,8,128]{0,2,1:T(8,128)(2,1)S(1)} %bitcast.260, bf16[384,1,128]{2,0,1:T(8,128)(2,1)S(1)} %copy-done.5, bf16[1024,1,128]{2,0,1:T(8,128)(2,1)S(1)} %bitcast.264), kind=kOutput, calls=%fused_computation.19 | convolution fusion | flops 1120990208 | bytes 19001344 | tf_op jit(solution)/shard_map/mkgd,nkd->kgmn/dot_general | solution.py:37
  297.4 9.4 %fusion.12 = f32[8,384]{1,0:T(8,128)S(1)} fusion(f32[1408,384,8]{1,0,2:T(8,128)} %get-tuple-element.38, f32[8,384]{1,0:T(8,128)S(1)} %get-tuple-element.37, pred[384,1408]{0,1:T(8,128)(4,1)S(1)} %pad_add_fusion), kind=kLoop, calls=%fused_computation.22 | loop fusion | flops 17298432 | bytes 17866752 | tf_op jit(solution)/shard_map/reduce_sum | solution.py:42
  306.8 9.7 %fusion.39 = bf16[384,1,8,128]{0,3,2,1:T(8,128)(2,1)S(1)} fusion(f32[1408,384,8]{1,0,2:T(8,128)} %get-tuple-element.38, f32[8,384]{1,0:T(8,128)S(1)} %get-tuple-element.37, pred[384,1408]{0,1:T(8,128)(4,1)S(1)} %pad_add_fusion, f32[384,8]{0,1:T(8,128)S(1)} %bitcast.280, bf16[384,1,128]{0,2,1:T(8,128)(2,1)S(1)} %copy-done.7, bf16[1024,1,128]{0,2,1:T(8,128)(2,1)S(1)} %copy.124), kind=kOutput, calls=%fused_computation.55 | convolution fusion | flops 1126105088 | bytes 19013632 | tf_op jit(solution)/shard_map/kgmn,nkd->mkgd/dot_general | solution.py:44
  318.0 5.6 %dynamic_update_slice.12 = bf16[1024,1024]{1,0:T(8,128)(2,1)S(1)} dynamic-update-slice(bf16[1024,1024]{1,0:T(8,128)(2,1)S(1)} %broadcast_in_dim.152, bf16[384,1024]{1,0:T(8,128)(2,1)} %broadcast_select_fusion.2, s32[]{:T(128)S(6)} %select_n.157, s32[]{:T(128)} %constant.116.clone.1) | dynamic-update-slice | bytes 1572868 | tf_op jit(solution)/shard_map/dynamic_update_slice | solution.py:107
  326.0 5.5 %dynamic_update_slice.13 = bf16[1024,1024]{1,0:T(8,128)(2,1)S(1)} dynamic-update-slice(bf16[1024,1024]{1,0:T(8,128)(2,1)S(1)} %dynamic_update_slice.12, bf16[384,1024]{1,0:T(8,128)(2,1)} %dynamic-slice_select_fusion.2, s32[]{:T(128)S(6)} %select_n.164, s32[]{:T(128)} %constant.116.clone.1) | dynamic-update-slice | bytes 1572868 | tf_op jit(solution)/shard_map/dynamic_update_slice | solution.py:107
  333.9 5.5 %dynamic_update_slice.14 = bf16[1024,1024]{1,0:T(8,128)(2,1)S(1)} dynamic-update-slice(bf16[1024,1024]{1,0:T(8,128)(2,1)S(1)} %dynamic_update_slice.13, bf16[384,1024]{1,0:T(8,128)(2,1)} %dynamic-slice_select_fusion.1, s32[]{:T(128)S(6)} %select_n.169, s32[]{:T(128)} %constant.116.clone.1) | dynamic-update-slice | bytes 1572868 | tf_op jit(solution)/shard_map/dynamic_update_slice | solution.py:107
  341.0 4.7 %dynamic_update_slice.15 = bf16[1024,1024]{1,0:T(8,128)(2,1)} dynamic-update-slice(bf16[1024,1024]{1,0:T(8,128)(2,1)} %copy-done, bf16[384,1024]{1,0:T(8,128)(2,1)} %dynamic-slice_select_fusion, s32[]{:T(128)S(6)} %select_n.174, s32[]{:T(128)} %constant.116.clone.1) | dynamic-update-slice | bytes 1572868 | tf_op jit(solution)/shard_map/dynamic_update_slice | solution.py:107
  (105 shorter events, 53.8 us)
Async XLA Ops:
  27.4 58.5 %copy-start.11 = (s32[1,4]{1,0:T(1,128)S(1)}, s32[1,4]{1,0:T(1,128)}, u32[]{:S(2)}) copy-start(s32[1,4]{1,0:T(1,128)} %param.13) | copy-start | bytes 52
  27.4 62.0 %copy-start.1 = (bf16[1024,1024]{1,0:T(8,128)(2,1)S(1)}, bf16[1024,1024]{1,0:T(8,128)(2,1)}, u32[]{:S(2)}) copy-start(bf16[1024,1024]{1,0:T(8,128)(2,1)} %param.7) | copy-start | bytes 6291460
  27.4 53.5 %all-to-all-start.2 = ((bf16[8,2,128,1024]{3,2,1,0:T(8,128)(2,1)}), bf16[8,2,128,1024]{3,2,1,0:T(8,128)(2,1)}, u32[]{:S(2)}, u32[]{:S(2)}) async-start(bf16[8,2,128,1024]{3,2,1,0:T(8,128)(2,1)} %stack.2), calls=%async_computation.2 | async-start | bytes 8388608 | tf_op jit(solution)/shard_map/all_to_all | solution.py:58
  32.5 61.3 %copy-start.10 = (s32[4,8]{1,0:T(4,128)S(1)}, s32[4,8]{1,0:T(4,128)}, u32[]{:S(2)}) copy-start(s32[4,8]{1,0:T(4,128)} %param.10) | copy-start | bytes 388
  32.9 66.5 %copy-start.12 = (s32[4]{0:T(128)S(1)}, s32[4]{0:T(128)}, u32[]{:S(2)}) copy-start(s32[4]{0:T(128)} %param.12) | copy-start | bytes 52
  80.9 102.0 %all-to-all-start.1 = ((bf16[32,2,2,128,128]{4,3,2,1,0:T(8,128)(2,1)}), bf16[32,2,2,128,128]{4,3,2,1,0:T(8,128)(2,1)}, u32[]{:S(2)}, u32[]{:S(2)}) async-start(bf16[32,2,2,128,128]{4,3,2,1,0:T(8,128)(2,1)} %broadcast_select_fusion), calls=%async_computation.1 | async-start | bytes 8388608 | tf_op jit(solution)/shard_map/all_to_all | solution.py:62
  226.3 19.4 %copy-start.9 = (bf16[384,1,128]{0,2,1:T(8,128)(2,1)S(1)}, bf16[384,1,128]{0,2,1:T(8,128)(2,1)}, u32[]{:S(2)}) copy-start(bf16[384,1,128]{0,2,1:T(8,128)(2,1)} %copy.105) | copy-start | bytes 294916
  245.7 13.4 %copy-start.4 = (bf16[1,8,1,128,128]{4,3,2,1,0:T(8,128)(2,1)S(1)}, bf16[1,8,1,128,128]{4,3,2,1,0:T(8,128)(2,1)}, u32[]{:S(2)}) copy-start(bf16[1,8,1,128,128]{4,3,2,1,0:T(8,128)(2,1)} %get-tuple-element.18) | copy-start | bytes 786436
  245.7 14.3 %copy-start.6 = (bf16[384,1,128]{2,0,1:T(8,128)(2,1)S(1)}, bf16[384,1,128]{2,0,1:T(8,128)(2,1)}, u32[]{:S(2)}) copy-start(bf16[384,1,128]{2,0,1:T(8,128)(2,1)} %get-tuple-element.11) | copy-start | bytes 294916
  268.8 9.5 %copy-start.8 = (bf16[384,1,128]{0,2,1:T(8,128)(2,1)S(1)}, bf16[384,1,128]{0,2,1:T(8,128)(2,1)}, u32[]{:S(2)}) copy-start(bf16[384,1,128]{0,2,1:T(8,128)(2,1)} %copy.99) | copy-start | bytes 294916
  278.3 11.0 %copy-start.3 = (bf16[1,8,1,128,128]{4,3,2,1,0:T(8,128)(2,1)S(1)}, bf16[1,8,1,128,128]{4,3,2,1,0:T(8,128)(2,1)}, u32[]{:S(2)}) copy-start(bf16[1,8,1,128,128]{4,3,2,1,0:T(8,128)(2,1)} %get-tuple-element.20) | copy-start | bytes 786436
  278.3 11.1 %copy-start.5 = (bf16[384,1,128]{2,0,1:T(8,128)(2,1)S(1)}, bf16[384,1,128]{2,0,1:T(8,128)(2,1)}, u32[]{:S(2)}) copy-start(bf16[384,1,128]{2,0,1:T(8,128)(2,1)} %get-tuple-element.12) | copy-start | bytes 294916
  289.4 17.4 %copy-start.7 = (bf16[384,1,128]{0,2,1:T(8,128)(2,1)S(1)}, bf16[384,1,128]{0,2,1:T(8,128)(2,1)}, u32[]{:S(2)}) copy-start(bf16[384,1,128]{0,2,1:T(8,128)(2,1)} %copy.93) | copy-start | bytes 294916
  306.8 32.7 %copy-start.2 = (bf16[384,1024]{1,0:T(8,128)(2,1)S(1)}, bf16[384,1024]{1,0:T(8,128)(2,1)}, u32[]{:S(2)}) copy-start(bf16[384,1024]{1,0:T(8,128)(2,1)} %copy.115) | copy-start | bytes 2359300
  339.4 1.6 copy-start
